TPU v7x, 32 devices: a whole 2x2x4 slice. The times are simulated.
32 devices in a mesh: sec: 8 (over y, x, core), cross: 4 (over z).
Axes of the slice: x: 2, y: 2, z: 4, core: 2. Of those that a mesh axis runs over, the one named last changes fastest.
Arguments:
- rhs_field: float32 [2, 8, 2, 512, 512], P(None, 'sec', None, 'cross'), may hold values from -1.5 to 1.5
- slowness: float32 [8, 512, 512], P('sec', 'cross'), may hold values from 0.25 to 4
- absorb_depth: int32 [8], P('sec'), may hold values from 8 to 64
- line_inverse: bfloat16 [8, 2, 512, 512], P('sec'), may hold values from -1 to 1
- cross_inverse: bfloat16 [8, 2, 512, 512], P('sec', None, 'cross'), may hold values from -1 to 1
Outputs:
- solution: float32 [2, 8, 2, 512, 512], P(None, 'sec', None, 'cross')
- residual: float32 [2, 8, 2, 512, 512], P(None, 'sec', None, 'cross')
All inputs are finite; a program needn't handle non-finite values.
Results may differ from a plain program's by a relative error of at most 0.02.
Values may be sent and summed in bfloat16 or wider, within the bound.
A program may use at most 64 MiB of HBM per device.

v0:
```python
import jax
import jax.numpy as jnp
from jax import lax
from jax.sharding import PartitionSpec as P

SIGMA_TOP = 2.0
CENTER = 128.0 / 30.0
FACE = 14.0 / 30.0
EDGE = 3.0 / 30.0
CORNER = 1.0 / 30.0


def passed_along(shard, axis, by):
    devices = lax.axis_size(axis)
    pairs = [(i, i + by) for i in range(devices) if 0 <= i + by < devices]
    return lax.ppermute(shard, axis, pairs)


def with_halo(cells, sides, width):
    for axis, dim in sides:
        count = lax.axis_size(axis)
        ends = count - 1
        head = lax.slice_in_dim(cells, 0, width, axis=dim)
        tail = lax.slice_in_dim(cells, cells.shape[dim] - width, cells.shape[dim], axis=dim)
        cells = jnp.concatenate(
            [
                lax.ppermute(tail, axis, [(i, (i + 1) % count) for i in range(ends)]),
                cells,
                lax.ppermute(head, axis, [((i + 1) % count, i) for i in range(ends)]),
            ],
            axis=dim,
        )
    return cells


def complex_line(source, matrix):
    real_part = jnp.dot(source[0], matrix[0], preferred_element_type=jnp.float32) - jnp.dot(
        source[1], matrix[1], preferred_element_type=jnp.float32
    )
    imag_part = jnp.dot(source[0], matrix[1], preferred_element_type=jnp.float32) + jnp.dot(
        source[1], matrix[0], preferred_element_type=jnp.float32
    )
    return jnp.stack([real_part, imag_part]).astype(jnp.bfloat16)


def cross_fold(mixed, coupling_rows):
    gathered = lax.all_gather(mixed, "cross", axis=2, tiled=True)
    real_real = jnp.einsum(
        "yk,rkx->ryx", coupling_rows[0], gathered[0], preferred_element_type=jnp.float32
    )
    imag_imag = jnp.einsum(
        "yk,rkx->ryx", coupling_rows[1], gathered[1], preferred_element_type=jnp.float32
    )
    real_imag = jnp.einsum(
        "yk,rkx->ryx", coupling_rows[0], gathered[1], preferred_element_type=jnp.float32
    )
    imag_real = jnp.einsum(
        "yk,rkx->ryx", coupling_rows[1], gathered[0], preferred_element_type=jnp.float32
    )
    real_part = real_real - imag_imag
    imag_part = real_imag + imag_real
    return jnp.stack([real_part, imag_part])


def sweep_section(rhs_local, prior, line_matrix, cross_local):
    item_count = rhs_local.shape[2]
    line_count = rhs_local.shape[3]
    column_count = rhs_local.shape[4]
    source = (rhs_local[:, 0] + prior).astype(jnp.bfloat16)
    mixed = complex_line(source.reshape(2, item_count * line_count, column_count), line_matrix)
    mixed = mixed.reshape(2, item_count, line_count, column_count)
    prior = cross_fold(mixed, cross_local[0])
    outputs = [prior]
    return jnp.stack(outputs, axis=1)


def absorption(absorb_depth, column_count):
    column = jnp.arange(column_count, dtype=jnp.int32)
    distance = jnp.minimum(column, column_count - 1 - column).astype(jnp.float32)
    depth = absorb_depth.astype(jnp.float32)[:, None]
    ramp = jnp.maximum(depth - distance[None, :], 0.0) / depth
    return SIGMA_TOP * ramp * ramp


def operate(field, padded, slowness, absorb_depth):
    layer_count = field.shape[1]
    line_count = field.shape[3]
    column_count = field.shape[4]
    weights = (0.0, FACE, EDGE, CORNER)
    near = jnp.zeros(field.shape, jnp.float32)
    for depth_move in (-1, 0, 1):
        for line_move in (-1, 0, 1):
            for column_move in (-1, 0, 1):
                reach = abs(depth_move) + abs(line_move) + abs(column_move)
                if reach > 0:
                    near = (
                        near
                        + weights[reach]
                        * padded[
                            :,
                            1 + depth_move : 1 + depth_move + layer_count,
                            :,
                            1 + line_move : 1 + line_move + line_count,
                            1 + column_move : 1 + column_move + column_count,
                        ]
                    )
    damping = absorption(absorb_depth, column_count)
    wave_real = slowness[:, None, :, :]
    wave_imag = wave_real * damping[:, None, None, :]
    real_part = CENTER * field[0] - near[0] - (wave_real * field[0] - wave_imag * field[1])
    imag_part = CENTER * field[1] - near[1] - (wave_real * field[1] + wave_imag * field[0])
    return jnp.stack([real_part, imag_part])


def per_device(rhs_field, slowness, absorb_depth, line_inverse, cross_inverse):
    line_matrix = line_inverse[0]
    layer_count = rhs_field.shape[1]
    item_count = rhs_field.shape[2]
    line_count = rhs_field.shape[3]
    column_count = rhs_field.shape[4]
    sections = lax.axis_size("sec")
    start_prior = jnp.zeros((2, item_count, line_count, column_count), jnp.float32)
    first = sweep_section(rhs_field, start_prior, line_matrix, cross_inverse)

    def advance_whole(counter, current):
        prior = passed_along(current[:, layer_count - 1].astype(jnp.bfloat16), "sec", 1).astype(
            jnp.float32
        )
        return sweep_section(rhs_field, prior, line_matrix, cross_inverse)

    solution = lax.fori_loop(0, sections - 1, advance_whole, first)
    padded = with_halo(solution.astype(jnp.bfloat16), (("sec", 1), ("cross", 3)), 1).astype(
        solution.dtype
    )
    padded = jnp.pad(padded, ((0, 0), (0, 0), (0, 0), (0, 0), (1, 1)))
    residual = rhs_field - operate(solution, padded, slowness, absorb_depth)
    return (solution, residual)


def solution(mesh):
    placed = (
        P(None, "sec", None, "cross", None),
        P("sec", "cross", None),
        P("sec"),
        P("sec", None, None, None),
        P("sec", None, "cross", None),
    )
    return jax.shard_map(
        per_device,
        mesh=mesh,
        in_specs=placed,
        out_specs=(P(None, "sec", None, "cross", None), P(None, "sec", None, "cross", None)),
        check_vma=False,
    )
```

profile of v0, /device:TPU:1, one launch (start us, length us, event | category | flops | bytes accessed | tf_op | source)
XLA Modules:
  0.0 556.7 jit_solution(8735741020299506886)
XLA Ops:
  13.2 46.5 %all-gather.3.cloned.1.call-done = bf16[2,2,512,512]{2,3,1,0:T(8,128)(2,1)} async-done(((bf16[2,2,128,512]{2,3,1,0:T(8,128)(2,1)}), bf16[2,2,512,512]{2,3,1,0:T(8,128)(2,1)}) %all-gather.3.cloned.1.call-update) | async-done | bytes 2097168 | tf_op jit(solution)/shard_map/all_gather | solution.py:47
  59.7 1.8 fusion.72
  64.2 452.2 %while.10 = (s32[]{:T(128)}, f32[2,1,2,128,512]{3,4,2,0,1:T(8,128)S(1)}, f32[2,1,2,128,512]{3,4,2,0,1:T(8,128)S(1)}, bf16[2,512,512]{2,1,0:T(8,128)(2,1)S(1)}, bf16[1,2,128,512]{3,2,1,0:T(8,128)(2,1)}, /*index=5*/s32[]{:T(128)}) while((s32[]{:T(128)}, f32[2,1,2,128,512]{3,4,2,0,1:T(8,128)S(1)}, f32[2,1,2,128,512]{3,4,2,0,1:T(8,128)S(1)}, ...), condition=%wide.region_1.0_spmd, body=%wide.region_0.0_spmd.sunk | while | flops 1075838976 | bytes 44040396 | solution.py:131
  65.2 5.2 collective-permute-start
  70.8 6.1 %collective-permute-done = bf16[2,2,128,512]{3,2,1,0:T(8,128)(2,1)} collective-permute-done((bf16[2,2,128,512]{3,2,1,0:T(8,128)(2,1)}, bf16[2,2,128,512]{3,2,1,0:T(8,128)(2,1)}, u32[]{:S(2)}, u32[]{:S(2)}) %collective-permute-start) | collective-permute-done | bytes 524320 | tf_op jit(solution)/shard_map/while/body/eval_jaxpr/ppermute | solution.py:16
  80.6 43.7 %all-gather.5.cloned.1.call-done = bf16[2,2,512,512]{2,3,1,0:T(8,128)(2,1)} async-done(((bf16[2,2,128,512]{2,3,1,0:T(8,128)(2,1)}), bf16[2,2,512,512]{2,3,1,0:T(8,128)(2,1)}) %all-gather.5.cloned.1.call-update) | async-done | bytes 2097168 | tf_op jit(solution)/shard_map/while/body/eval_jaxpr/all_gather | solution.py:47
  124.3 1.8 fusion.150
  129.8 5.2 collective-permute-start
  135.4 6.1 %collective-permute-done = bf16[2,2,128,512]{3,2,1,0:T(8,128)(2,1)} collective-permute-done((bf16[2,2,128,512]{3,2,1,0:T(8,128)(2,1)}, bf16[2,2,128,512]{3,2,1,0:T(8,128)(2,1)}, u32[]{:S(2)}, u32[]{:S(2)}) %collective-permute-start) | collective-permute-done | bytes 524320 | tf_op jit(solution)/shard_map/while/body/eval_jaxpr/ppermute | solution.py:16
  145.2 43.7 %all-gather.5.cloned.1.call-done = bf16[2,2,512,512]{2,3,1,0:T(8,128)(2,1)} async-done(((bf16[2,2,128,512]{2,3,1,0:T(8,128)(2,1)}), bf16[2,2,512,512]{2,3,1,0:T(8,128)(2,1)}) %all-gather.5.cloned.1.call-update) | async-done | bytes 2097168 | tf_op jit(solution)/shard_map/while/body/eval_jaxpr/all_gather | solution.py:47
  188.9 1.8 fusion.150
  194.4 5.2 collective-permute-start
  200.0 6.1 %collective-permute-done = bf16[2,2,128,512]{3,2,1,0:T(8,128)(2,1)} collective-permute-done((bf16[2,2,128,512]{3,2,1,0:T(8,128)(2,1)}, bf16[2,2,128,512]{3,2,1,0:T(8,128)(2,1)}, u32[]{:S(2)}, u32[]{:S(2)}) %collective-permute-start) | collective-permute-done | bytes 524320 | tf_op jit(solution)/shard_map/while/body/eval_jaxpr/ppermute | solution.py:16
  209.8 43.7 %all-gather.5.cloned.1.call-done = bf16[2,2,512,512]{2,3,1,0:T(8,128)(2,1)} async-done(((bf16[2,2,128,512]{2,3,1,0:T(8,128)(2,1)}), bf16[2,2,512,512]{2,3,1,0:T(8,128)(2,1)}) %all-gather.5.cloned.1.call-update) | async-done | bytes 2097168 | tf_op jit(solution)/shard_map/while/body/eval_jaxpr/all_gather | solution.py:47
  259.0 5.2 collective-permute-start
  264.6 6.1 %collective-permute-done = bf16[2,2,128,512]{3,2,1,0:T(8,128)(2,1)} collective-permute-done((bf16[2,2,128,512]{3,2,1,0:T(8,128)(2,1)}, bf16[2,2,128,512]{3,2,1,0:T(8,128)(2,1)}, u32[]{:S(2)}, u32[]{:S(2)}) %collective-permute-start) | collective-permute-done | bytes 524320 | tf_op jit(solution)/shard_map/while/body/eval_jaxpr/ppermute | solution.py:16
  274.4 43.7 %all-gather.5.cloned.1.call-done = bf16[2,2,512,512]{2,3,1,0:T(8,128)(2,1)} async-done(((bf16[2,2,128,512]{2,3,1,0:T(8,128)(2,1)}), bf16[2,2,512,512]{2,3,1,0:T(8,128)(2,1)}) %all-gather.5.cloned.1.call-update) | async-done | bytes 2097168 | tf_op jit(solution)/shard_map/while/body/eval_jaxpr/all_gather | solution.py:47
  323.6 5.2 collective-permute-start
  329.2 6.1 %collective-permute-done = bf16[2,2,128,512]{3,2,1,0:T(8,128)(2,1)} collective-permute-done((bf16[2,2,128,512]{3,2,1,0:T(8,128)(2,1)}, bf16[2,2,128,512]{3,2,1,0:T(8,128)(2,1)}, u32[]{:S(2)}, u32[]{:S(2)}) %collective-permute-start) | collective-permute-done | bytes 524320 | tf_op jit(solution)/shard_map/while/body/eval_jaxpr/ppermute | solution.py:16
  339.0 43.7 %all-gather.5.cloned.1.call-done = bf16[2,2,512,512]{2,3,1,0:T(8,128)(2,1)} async-done(((bf16[2,2,128,512]{2,3,1,0:T(8,128)(2,1)}), bf16[2,2,512,512]{2,3,1,0:T(8,128)(2,1)}) %all-gather.5.cloned.1.call-update) | async-done | bytes 2097168 | tf_op jit(solution)/shard_map/while/body/eval_jaxpr/all_gather | solution.py:47
  388.2 5.2 collective-permute-start
  393.8 6.1 %collective-permute-done = bf16[2,2,128,512]{3,2,1,0:T(8,128)(2,1)} collective-permute-done((bf16[2,2,128,512]{3,2,1,0:T(8,128)(2,1)}, bf16[2,2,128,512]{3,2,1,0:T(8,128)(2,1)}, u32[]{:S(2)}, u32[]{:S(2)}) %collective-permute-start) | collective-permute-done | bytes 524320 | tf_op jit(solution)/shard_map/while/body/eval_jaxpr/ppermute | solution.py:16
  403.6 43.7 %all-gather.5.cloned.1.call-done = bf16[2,2,512,512]{2,3,1,0:T(8,128)(2,1)} async-done(((bf16[2,2,128,512]{2,3,1,0:T(8,128)(2,1)}), bf16[2,2,512,512]{2,3,1,0:T(8,128)(2,1)}) %all-gather.5.cloned.1.call-update) | async-done | bytes 2097168 | tf_op jit(solution)/shard_map/while/body/eval_jaxpr/all_gather | solution.py:47
  452.8 5.2 collective-permute-start
  458.4 6.1 %collective-permute-done = bf16[2,2,128,512]{3,2,1,0:T(8,128)(2,1)} collective-permute-done((bf16[2,2,128,512]{3,2,1,0:T(8,128)(2,1)}, bf16[2,2,128,512]{3,2,1,0:T(8,128)(2,1)}, u32[]{:S(2)}, u32[]{:S(2)}) %collective-permute-start) | collective-permute-done | bytes 524320 | tf_op jit(solution)/shard_map/while/body/eval_jaxpr/ppermute | solution.py:16
  468.2 43.7 %all-gather.5.cloned.1.call-done = bf16[2,2,512,512]{2,3,1,0:T(8,128)(2,1)} async-done(((bf16[2,2,128,512]{2,3,1,0:T(8,128)(2,1)}), bf16[2,2,512,512]{2,3,1,0:T(8,128)(2,1)}) %all-gather.5.cloned.1.call-update) | async-done | bytes 2097168 | tf_op jit(solution)/shard_map/while/body/eval_jaxpr/all_gather | solution.py:47
  516.8 5.4 collective-permute-start.1
  522.2 1.9 collective-permute-start.2
  524.8 3.5 collective-permute-done.1
  528.3 7.2 %collective-permute-done.2 = bf16[2,1,2,128,512]{4,3,2,1,0:T(8,128)(2,1)S(1)} collective-permute-done((bf16[2,1,2,128,512]{4,3,2,1,0:T(8,128)(2,1)S(1)}, bf16[2,1,2,128,512]{4,3,2,1,0:T(8,128)(2,1)S(1)}, u32[]{:S(2)}, u32[]{:S(2)}) %collective-permute-start.2) | collective-permute-done | bytes 524320 | tf_op jit(solution)/shard_map/ppermute | solution.py:29
  538.2 3.2 collective-permute-done.4
  542.0 5.4 fusion.68
  (193 shorter events, 76.7 us)
Async XLA Ops:
  7.2 52.6 %all-gather.3.cloned.1.call-start = ((), (), s32[]{:S(2)}) async-start(), calls=%async_computation | async-start | bytes 2621440 | tf_op jit(solution)/shard_map/all_gather | solution.py:47
  10.8 48.9 %copy-start.2 = (bf16[1,2,128,512]{3,2,1,0:T(8,128)(2,1)S(1)}, bf16[1,2,128,512]{3,2,1,0:T(8,128)(2,1)}, u32[]{:S(2)}) copy-start(bf16[1,2,128,512]{3,2,1,0:T(8,128)(2,1)} %param.11) | copy-start | bytes 786436
  64.2 60.2 %all-gather.5.cloned.1.call-start = ((), (), s32[]{:S(2)}) async-start(), calls=%async_computation.1 | async-start | bytes 2621440 | tf_op jit(solution)/shard_map/while/body/eval_jaxpr/all_gather | solution.py:47
  65.2 11.7 %collective-permute-start = (bf16[2,2,128,512]{3,2,1,0:T(8,128)(2,1)}, bf16[2,2,128,512]{3,2,1,0:T(8,128)(2,1)}, u32[]{:S(2)}, u32[]{:S(2)}) collective-permute-start(bf16[2,2,128,512]{3,2,1,0:T(8,128)(2,1)} %bitcast.168), channel_id=1, source_target_pairs={{0,4},{4,8},{8,12},{12,16},{16,20},{20,24},{24,28},{1,5},{5,9},{9,... | collective-permute-start | bytes 1572872 | tf_op jit(solution)/shard_map/while/body/eval_jaxpr/ppermute | solution.py:16
  79.5 44.8 %copy-start.3 = (bf16[1,2,128,512]{3,2,1,0:T(8,128)(2,1)S(1)}, bf16[1,2,128,512]{3,2,1,0:T(8,128)(2,1)}, u32[]{:S(2)}) copy-start(bf16[1,2,128,512]{3,2,1,0:T(8,128)(2,1)} %get-tuple-element.113) | copy-start | bytes 786436 | tf_op jit(solution)/shard_map/while
  124.3 3.5 copy-start.1
  128.8 60.2 %all-gather.5.cloned.1.call-start = ((), (), s32[]{:S(2)}) async-start(), calls=%async_computation.1 | async-start | bytes 2621440 | tf_op jit(solution)/shard_map/while/body/eval_jaxpr/all_gather | solution.py:47
  129.8 11.7 %collective-permute-start = (bf16[2,2,128,512]{3,2,1,0:T(8,128)(2,1)}, bf16[2,2,128,512]{3,2,1,0:T(8,128)(2,1)}, u32[]{:S(2)}, u32[]{:S(2)}) collective-permute-start(bf16[2,2,128,512]{3,2,1,0:T(8,128)(2,1)} %bitcast.168), channel_id=1, source_target_pairs={{0,4},{4,8},{8,12},{12,16},{16,20},{20,24},{24,28},{1,5},{5,9},{9,... | collective-permute-start | bytes 1572872 | tf_op jit(solution)/shard_map/while/body/eval_jaxpr/ppermute | solution.py:16
  144.1 44.8 %copy-start.3 = (bf16[1,2,128,512]{3,2,1,0:T(8,128)(2,1)S(1)}, bf16[1,2,128,512]{3,2,1,0:T(8,128)(2,1)}, u32[]{:S(2)}) copy-start(bf16[1,2,128,512]{3,2,1,0:T(8,128)(2,1)} %get-tuple-element.113) | copy-start | bytes 786436 | tf_op jit(solution)/shard_map/while
  193.4 60.2 %all-gather.5.cloned.1.call-start = ((), (), s32[]{:S(2)}) async-start(), calls=%async_computation.1 | async-start | bytes 2621440 | tf_op jit(solution)/shard_map/while/body/eval_jaxpr/all_gather | solution.py:47
  194.4 11.7 %collective-permute-start = (bf16[2,2,128,512]{3,2,1,0:T(8,128)(2,1)}, bf16[2,2,128,512]{3,2,1,0:T(8,128)(2,1)}, u32[]{:S(2)}, u32[]{:S(2)}) collective-permute-start(bf16[2,2,128,512]{3,2,1,0:T(8,128)(2,1)} %bitcast.168), channel_id=1, source_target_pairs={{0,4},{4,8},{8,12},{12,16},{16,20},{20,24},{24,28},{1,5},{5,9},{9,... | collective-permute-start | bytes 1572872 | tf_op jit(solution)/shard_map/while/body/eval_jaxpr/ppermute | solution.py:16
  208.7 44.8 %copy-start.3 = (bf16[1,2,128,512]{3,2,1,0:T(8,128)(2,1)S(1)}, bf16[1,2,128,512]{3,2,1,0:T(8,128)(2,1)}, u32[]{:S(2)}) copy-start(bf16[1,2,128,512]{3,2,1,0:T(8,128)(2,1)} %get-tuple-element.113) | copy-start | bytes 786436 | tf_op jit(solution)/shard_map/while
  253.5 3.5 copy-start.1
  258.0 60.2 %all-gather.5.cloned.1.call-start = ((), (), s32[]{:S(2)}) async-start(), calls=%async_computation.1 | async-start | bytes 2621440 | tf_op jit(solution)/shard_map/while/body/eval_jaxpr/all_gather | solution.py:47
  259.0 11.7 %collective-permute-start = (bf16[2,2,128,512]{3,2,1,0:T(8,128)(2,1)}, bf16[2,2,128,512]{3,2,1,0:T(8,128)(2,1)}, u32[]{:S(2)}, u32[]{:S(2)}) collective-permute-start(bf16[2,2,128,512]{3,2,1,0:T(8,128)(2,1)} %bitcast.168), channel_id=1, source_target_pairs={{0,4},{4,8},{8,12},{12,16},{16,20},{20,24},{24,28},{1,5},{5,9},{9,... | collective-permute-start | bytes 1572872 | tf_op jit(solution)/shard_map/while/body/eval_jaxpr/ppermute | solution.py:16
  273.3 44.8 %copy-start.3 = (bf16[1,2,128,512]{3,2,1,0:T(8,128)(2,1)S(1)}, bf16[1,2,128,512]{3,2,1,0:T(8,128)(2,1)}, u32[]{:S(2)}) copy-start(bf16[1,2,128,512]{3,2,1,0:T(8,128)(2,1)} %get-tuple-element.113) | copy-start | bytes 786436 | tf_op jit(solution)/shard_map/while
  322.6 60.2 %all-gather.5.cloned.1.call-start = ((), (), s32[]{:S(2)}) async-start(), calls=%async_computation.1 | async-start | bytes 2621440 | tf_op jit(solution)/shard_map/while/body/eval_jaxpr/all_gather | solution.py:47
  323.6 11.7 %collective-permute-start = (bf16[2,2,128,512]{3,2,1,0:T(8,128)(2,1)}, bf16[2,2,128,512]{3,2,1,0:T(8,128)(2,1)}, u32[]{:S(2)}, u32[]{:S(2)}) collective-permute-start(bf16[2,2,128,512]{3,2,1,0:T(8,128)(2,1)} %bitcast.168), channel_id=1, source_target_pairs={{0,4},{4,8},{8,12},{12,16},{16,20},{20,24},{24,28},{1,5},{5,9},{9,... | collective-permute-start | bytes 1572872 | tf_op jit(solution)/shard_map/while/body/eval_jaxpr/ppermute | solution.py:16
  337.9 44.8 %copy-start.3 = (bf16[1,2,128,512]{3,2,1,0:T(8,128)(2,1)S(1)}, bf16[1,2,128,512]{3,2,1,0:T(8,128)(2,1)}, u32[]{:S(2)}) copy-start(bf16[1,2,128,512]{3,2,1,0:T(8,128)(2,1)} %get-tuple-element.113) | copy-start | bytes 786436 | tf_op jit(solution)/shard_map/while
  387.2 60.2 %all-gather.5.cloned.1.call-start = ((), (), s32[]{:S(2)}) async-start(), calls=%async_computation.1 | async-start | bytes 2621440 | tf_op jit(solution)/shard_map/while/body/eval_jaxpr/all_gather | solution.py:47
  388.2 11.7 %collective-permute-start = (bf16[2,2,128,512]{3,2,1,0:T(8,128)(2,1)}, bf16[2,2,128,512]{3,2,1,0:T(8,128)(2,1)}, u32[]{:S(2)}, u32[]{:S(2)}) collective-permute-start(bf16[2,2,128,512]{3,2,1,0:T(8,128)(2,1)} %bitcast.168), channel_id=1, source_target_pairs={{0,4},{4,8},{8,12},{12,16},{16,20},{20,24},{24,28},{1,5},{5,9},{9,... | collective-permute-start | bytes 1572872 | tf_op jit(solution)/shard_map/while/body/eval_jaxpr/ppermute | solution.py:16
  402.5 44.8 %copy-start.3 = (bf16[1,2,128,512]{3,2,1,0:T(8,128)(2,1)S(1)}, bf16[1,2,128,512]{3,2,1,0:T(8,128)(2,1)}, u32[]{:S(2)}) copy-start(bf16[1,2,128,512]{3,2,1,0:T(8,128)(2,1)} %get-tuple-element.113) | copy-start | bytes 786436 | tf_op jit(solution)/shard_map/while
  451.8 60.2 %all-gather.5.cloned.1.call-start = ((), (), s32[]{:S(2)}) async-start(), calls=%async_computation.1 | async-start | bytes 2621440 | tf_op jit(solution)/shard_map/while/body/eval_jaxpr/all_gather | solution.py:47
  452.8 11.7 %collective-permute-start = (bf16[2,2,128,512]{3,2,1,0:T(8,128)(2,1)}, bf16[2,2,128,512]{3,2,1,0:T(8,128)(2,1)}, u32[]{:S(2)}, u32[]{:S(2)}) collective-permute-start(bf16[2,2,128,512]{3,2,1,0:T(8,128)(2,1)} %bitcast.168), channel_id=1, source_target_pairs={{0,4},{4,8},{8,12},{12,16},{16,20},{20,24},{24,28},{1,5},{5,9},{9,... | collective-permute-start | bytes 1572872 | tf_op jit(solution)/shard_map/while/body/eval_jaxpr/ppermute | solution.py:16
  467.1 44.8 %copy-start.3 = (bf16[1,2,128,512]{3,2,1,0:T(8,128)(2,1)S(1)}, bf16[1,2,128,512]{3,2,1,0:T(8,128)(2,1)}, u32[]{:S(2)}) copy-start(bf16[1,2,128,512]{3,2,1,0:T(8,128)(2,1)} %get-tuple-element.113) | copy-start | bytes 786436 | tf_op jit(solution)/shard_map/while
  511.9 3.5 copy-start.1
  516.7 30.7 %copy-start.6 = (f32[2,1,2,128,512]{4,3,2,1,0:T(8,128)}, f32[2,1,2,128,512]{4,3,2,1,0:T(8,128)S(1)}, u32[]{:S(2)}) copy-start(f32[2,1,2,128,512]{4,3,2,1,0:T(8,128)S(1)} %copy.26) | copy-start | bytes 3145732
  516.7 21.5 %copy-start.8 = (f32[1,128,512]{2,1,0:T(8,128)S(1)}, f32[1,128,512]{2,1,0:T(8,128)}, u32[]{:S(2)}) copy-start(f32[1,128,512]{2,1,0:T(8,128)} %param.8) | copy-start | bytes 786436
  516.8 11.5 %collective-permute-start.1 = (bf16[2,1,2,128,512]{4,3,2,1,0:T(8,128)(2,1)S(1)}, bf16[2,1,2,128,512]{4,3,2,1,0:T(8,128)(2,1)S(1)}, u32[]{:S(2)}, u32[]{:S(2)}) collective-permute-start(bf16[2,1,2,128,512]{4,3,2,1,0:T(8,128)(2,1)S(1)} %convert_element_type.40), channel_id=1, source_target_pairs={{0,4},{4,8},{8,12},{12,16},{16,20},{20,24},{24,28},{1,5},{5,9},{9,... | collective-permute-start | bytes 1572872 | tf_op jit(solution)/shard_map/ppermute | solution.py:27
  522.2 13.3 %collective-permute-start.2 = (bf16[2,1,2,128,512]{4,3,2,1,0:T(8,128)(2,1)S(1)}, bf16[2,1,2,128,512]{4,3,2,1,0:T(8,128)(2,1)S(1)}, u32[]{:S(2)}, u32[]{:S(2)}) collective-permute-start(bf16[2,1,2,128,512]{4,3,2,1,0:T(8,128)(2,1)S(1)} %convert_element_type.40), channel_id=1, source_target_pairs={{4,0},{8,4},{12,8},{16,12},{20,16},{24,20},{28,24},{5,1},{9,5},{13... | collective-permute-start | bytes 1572872 | tf_op jit(solution)/shard_map/ppermute | solution.py:29
  535.6 2.6 collective-permute-start.3
  536.9 4.6 collective-permute-start.4
  (8 other events, 23.4 us)
Sparse Core Ops, SparseCore 0:
  13.0 46.7 all-gather.2
  80.7 43.5 all-gather.4
  145.3 43.5 all-gather.4
  209.9 43.5 all-gather.4
  274.5 43.5 all-gather.4
  339.1 43.5 all-gather.4
  403.7 43.5 all-gather.4
  468.3 43.5 all-gather.4
where the time goes:
time: 558 us; the launch traced here: 557 us
  waiting for transfers between devices  409 us (73%)
  starting transfers between devices  46.9 us (8%)
  matrix products  44.8 us (8%)
  other arithmetic  24.7 us (4%)
  local copies, waits for them, and re-layouts  15 us (3%)
  between operations  14.9 us (3%)
    all_gather x8, waiting for transfers between devices, cross_fold(): gathered = lax.all_gather(mixed, 'cross', axis=2, tiled=True)  353 us
    ppermute x7, waiting for transfers between devices, passed_along(): return lax.ppermute(shard, axis, pairs)  42.6 us
    ppermute x7, starting transfers between devices, passed_along(): return lax.ppermute(shard, axis, pairs)  36.7 us
    dot_general x8, matrix products, cross_fold(): jnp.einsum('yk,rkx->ryx', coupling_rows[0], gathered[0], preferred_elemen...  14.4 us
    dot_general x8, matrix products, cross_fold(): jnp.einsum('yk,rkx->ryx', coupling_rows[0], gathered[1], preferred_elemen...  13.2 us
  transfers between devices with their start and end apart: 19, of which 18 were waited for; matrix products, arithmetic and copies ran while one was open for 0% of the time, Pallas kernels for 0%

commit v1 on v0

--- a/solution.py
+++ b/solution.py
@@ -44,7 +44,23 @@
 
 
 def cross_fold(mixed, coupling_rows):
-    gathered = lax.all_gather(mixed, "cross", axis=2, tiled=True)
+    carry_in, x_new, part_next = (lax.axis_size("cross"), lax.axis_index("cross"), mixed.shape[2])
+    trail = [(jj, (jj + 1) % carry_in) for jj in range(carry_in)]
+    gathered = jnp.zeros((*mixed.shape[:2], carry_in * part_next, *mixed.shape[3:]), mixed.dtype)
+    tray = [(jj, (jj - 1) % carry_in) for jj in range(carry_in)]
+    gathered = lax.dynamic_update_slice_in_dim(gathered, mixed, x_new * part_next, axis=2)
+    r2 = carry_in // 2
+    moved = piece_now = mixed
+    for idx in tuple(range(1, r2 + 1)):
+        moved = lax.ppermute(moved, "cross", trail)
+        gathered = lax.dynamic_update_slice_in_dim(
+            gathered, moved, (x_new - idx) % carry_in * part_next, axis=2
+        )
+        if idx < carry_in - r2:
+            piece_now = lax.ppermute(piece_now, "cross", perm=tray)
+            gathered = lax.dynamic_update_slice_in_dim(
+                gathered, piece_now, (x_new + idx) % carry_in * part_next, axis=2
+            )
     real_real = jnp.einsum(
         "yk,rkx->ryx", coupling_rows[0], gathered[0], preferred_element_type=jnp.float32
     )

time: 558 us -> 476 us (0.85)
  waiting for transfers between devices: 409 us -> 207 us
  starting transfers between devices: 46.9 us -> 141 us
  local copies, waits for them, and re-layouts: 15 us -> 66.2 us
  matrix products: 44.8 us -> 28.2 us
  between operations: 14.9 us -> 1.55 us
    all_gather x8 -> x0, waiting for transfers between devices: 353 us -> none  [cross_fold(): gathered = lax.all_gather(mixed, 'cross', axis=2, tiled=True)]
    ppermute x0 -> x24, waiting for transfers between devices: none -> 156 us  [the longest x16 122 us: cross_fold(): moved = lax.ppermute(moved, 'cross', trail)]
    ppermute x7, starting transfers between devices: 36.7 us -> 90 us  [passed_along(): return lax.ppermute(shard, axis, pairs)]
    ppermute x0 -> x24, starting transfers between devices: none -> 30.7 us  [the longest x8 24.9 us: cross_fold(): piece_now = lax.ppermute(piece_now, 'cross', perm=tray)]
    dynamic_update_slice x0 -> x24, local copies, waits for them, and re-layouts: none -> 30.4 us  [the longest x16 20.4 us: cross_fold(): lax.dynamic_update_slice_in_dim(gathered, moved, (x_new - idx) % carry_in...]
    while x28 -> x56, local copies, waits for them, and re-layouts: 0.07 us -> 13.5 us
    ppermute x2, starting transfers between devices: 6.67 us -> 17.4 us  [with_halo(): lax.ppermute(tail, axis, [(i, (i + 1) % count) for i in range(ends)])]
    dot_general x8, matrix products: 14.4 us -> 4.66 us  [cross_fold(): jnp.einsum('yk,rkx->ryx', coupling_rows[0], gathered[0], preferred_elemen...]
  transfers between devices with their start and end apart: 19 -> 35, of which waited for: 18 -> 33; matrix products, arithmetic and copies ran while one was open for 0% -> 5% of each run, Pallas kernels for 0% -> 0%
where the time goes in v1:
time: 476 us; the launch traced here: 471 us
  waiting for transfers between devices  207 us (43%)
  starting transfers between devices  141 us (30%)
  local copies, waits for them, and re-layouts  66.2 us (14%)
  matrix products  28.2 us (6%)
  other arithmetic  25.6 us (5%)
    ppermute x16, waiting for transfers between devices, cross_fold(): moved = lax.ppermute(moved, 'cross', trail)  122 us
    ppermute x7, starting transfers between devices, passed_along(): return lax.ppermute(shard, axis, pairs)  90 us
    ppermute x7, waiting for transfers between devices, passed_along(): return lax.ppermute(shard, axis, pairs)  42.4 us
    ppermute x8, waiting for transfers between devices, cross_fold(): piece_now = lax.ppermute(piece_now, 'cross', perm=tray)  33.8 us
    ppermute x8, starting transfers between devices, cross_fold(): piece_now = lax.ppermute(piece_now, 'cross', perm=tray)  24.9 us
    dynamic_update_slice x16, local copies, waits for them, and re-layouts, cross_fold(): lax.dynamic_update_slice_in_dim(gathered, moved, (x_new - idx) % carry_in...  20.4 us
    ppermute x2, starting transfers between devices, with_halo(): lax.ppermute(tail, axis, [(i, (i + 1) % count) for i in range(ends)])  17.4 us
    while x56, local copies, waits for them, and re-layouts  13.5 us
  transfers between devices with their start and end apart: 35, of which 33 were waited for; matrix products, arithmetic and copies ran while one was open for 5% of the time, Pallas kernels for 0%

profile of v1, /device:TPU:1, one launch (start us, length us, event | category | flops | bytes accessed | tf_op | source)
XLA Modules:
  0.0 470.8 jit_solution(690667223698637292)
XLA Ops:
  10.5 12.0 %collective-permute-done.4 = bf16[2,2,128,512]{2,3,1,0:T(8,128)(2,1)} collective-permute-done((bf16[2,2,128,512]{2,3,1,0:T(8,128)(2,1)}, bf16[2,2,128,512]{2,3,1,0:T(8,128)(2,1)}, u32[]{:S(2)}, u32[]{:S(2)}) %collective-permute-start.4) | collective-permute-done | bytes 524320 | tf_op jit(solution)/shard_map/ppermute | solution.py:55
  24.8 8.5 %collective-permute-done.5 = bf16[2,2,128,512]{2,3,1,0:T(8,128)(2,1)} collective-permute-done((bf16[2,2,128,512]{2,3,1,0:T(8,128)(2,1)}, bf16[2,2,128,512]{2,3,1,0:T(8,128)(2,1)}, u32[]{:S(2)}, u32[]{:S(2)}) %collective-permute-start.5) | collective-permute-done | bytes 524320 | tf_op jit(solution)/shard_map/ppermute | solution.py:60
  35.2 7.8 %collective-permute-done.6 = bf16[2,2,128,512]{2,3,1,0:T(8,128)(2,1)} collective-permute-done((bf16[2,2,128,512]{2,3,1,0:T(8,128)(2,1)}, bf16[2,2,128,512]{2,3,1,0:T(8,128)(2,1)}, u32[]{:S(2)}, u32[]{:S(2)}) %collective-permute-start.6) | collective-permute-done | bytes 524320 | tf_op jit(solution)/shard_map/ppermute | solution.py:55
  51.6 380.1 %while.12 = (s32[]{:T(128)}, f32[2,1,2,128,512]{3,4,2,0,1:T(8,128)S(1)}, f32[2,1,2,128,512]{3,4,2,0,1:T(8,128)S(1)}, bf16[2,512,512]{2,1,0:T(8,128)(2,1)S(1)}, b...) while((s32[]{:T(128)}, ...), condition=%wide.region_1.2_spmd, body=%wide.region_0.1_spmd.sunk | while | flops 1076625408 | bytes 49284048 | solution.py:147
  52.7 6.3 %collective-permute-start = (bf16[2,2,128,512]{3,2,1,0:T(8,128)(2,1)}, bf16[2,2,128,512]{3,2,1,0:T(8,128)(2,1)}, u32[]{:S(2)}, u32[]{:S(2)}) collective-permute-start(bf16[2,2,128,512]{3,2,1,0:T(8,128)(2,1)} %bitcast.168), channel_id=1, source_target_pairs={{0,4},{4,8},{8,12},{12,16},{16,20},{20,24},{24,28},{1,5},{5,9},{9,... | collective-permute-start | bytes 1572872 | tf_op jit(solution)/shard_map/while/body/eval_jaxpr/ppermute | solution.py:16
  59.4 6.1 %collective-permute-done = bf16[2,2,128,512]{3,2,1,0:T(8,128)(2,1)} collective-permute-done((bf16[2,2,128,512]{3,2,1,0:T(8,128)(2,1)}, bf16[2,2,128,512]{3,2,1,0:T(8,128)(2,1)}, u32[]{:S(2)}, u32[]{:S(2)}) %collective-permute-start) | collective-permute-done | bytes 524320 | tf_op jit(solution)/shard_map/while/body/eval_jaxpr/ppermute | solution.py:16
  74.1 12.8 %collective-permute-done.1 = bf16[2,2,128,512]{2,3,1,0:T(8,128)(2,1)} collective-permute-done((bf16[2,2,128,512]{2,3,1,0:T(8,128)(2,1)}, bf16[2,2,128,512]{2,3,1,0:T(8,128)(2,1)}, u32[]{:S(2)}, u32[]{:S(2)}) %collective-permute-start.1) | collective-permute-done | bytes 524320 | tf_op jit(solution)/shard_map/while/body/eval_jaxpr/ppermute | solution.py:55
  95.6 7.7 %collective-permute-done.3 = bf16[2,2,128,512]{2,3,1,0:T(8,128)(2,1)} collective-permute-done((bf16[2,2,128,512]{2,3,1,0:T(8,128)(2,1)}, bf16[2,2,128,512]{2,3,1,0:T(8,128)(2,1)}, u32[]{:S(2)}, u32[]{:S(2)}) %collective-permute-start.3) | collective-permute-done | bytes 524320 | tf_op jit(solution)/shard_map/while/body/eval_jaxpr/ppermute | solution.py:55
  108.5 9.5 %collective-permute-start = (bf16[2,2,128,512]{3,2,1,0:T(8,128)(2,1)}, bf16[2,2,128,512]{3,2,1,0:T(8,128)(2,1)}, u32[]{:S(2)}, u32[]{:S(2)}) collective-permute-start(bf16[2,2,128,512]{3,2,1,0:T(8,128)(2,1)} %bitcast.168), channel_id=1, source_target_pairs={{0,4},{4,8},{8,12},{12,16},{16,20},{20,24},{24,28},{1,5},{5,9},{9,... | collective-permute-start | bytes 1572872 | tf_op jit(solution)/shard_map/while/body/eval_jaxpr/ppermute | solution.py:16
  118.4 6.1 %collective-permute-done = bf16[2,2,128,512]{3,2,1,0:T(8,128)(2,1)} collective-permute-done((bf16[2,2,128,512]{3,2,1,0:T(8,128)(2,1)}, bf16[2,2,128,512]{3,2,1,0:T(8,128)(2,1)}, u32[]{:S(2)}, u32[]{:S(2)}) %collective-permute-start) | collective-permute-done | bytes 524320 | tf_op jit(solution)/shard_map/while/body/eval_jaxpr/ppermute | solution.py:16
  133.1 12.8 %collective-permute-done.1 = bf16[2,2,128,512]{2,3,1,0:T(8,128)(2,1)} collective-permute-done((bf16[2,2,128,512]{2,3,1,0:T(8,128)(2,1)}, bf16[2,2,128,512]{2,3,1,0:T(8,128)(2,1)}, u32[]{:S(2)}, u32[]{:S(2)}) %collective-permute-start.1) | collective-permute-done | bytes 524320 | tf_op jit(solution)/shard_map/while/body/eval_jaxpr/ppermute | solution.py:55
  150.6 6.3 %collective-permute-done.3 = bf16[2,2,128,512]{2,3,1,0:T(8,128)(2,1)} collective-permute-done((bf16[2,2,128,512]{2,3,1,0:T(8,128)(2,1)}, bf16[2,2,128,512]{2,3,1,0:T(8,128)(2,1)}, u32[]{:S(2)}, u32[]{:S(2)}) %collective-permute-start.3) | collective-permute-done | bytes 524320 | tf_op jit(solution)/shard_map/while/body/eval_jaxpr/ppermute | solution.py:55
  162.3 14.8 %collective-permute-start = (bf16[2,2,128,512]{3,2,1,0:T(8,128)(2,1)}, bf16[2,2,128,512]{3,2,1,0:T(8,128)(2,1)}, u32[]{:S(2)}, u32[]{:S(2)}) collective-permute-start(bf16[2,2,128,512]{3,2,1,0:T(8,128)(2,1)} %bitcast.168), channel_id=1, source_target_pairs={{0,4},{4,8},{8,12},{12,16},{16,20},{20,24},{24,28},{1,5},{5,9},{9,... | collective-permute-start | bytes 1572872 | tf_op jit(solution)/shard_map/while/body/eval_jaxpr/ppermute | solution.py:16
  177.4 6.1 %collective-permute-done = bf16[2,2,128,512]{3,2,1,0:T(8,128)(2,1)} collective-permute-done((bf16[2,2,128,512]{3,2,1,0:T(8,128)(2,1)}, bf16[2,2,128,512]{3,2,1,0:T(8,128)(2,1)}, u32[]{:S(2)}, u32[]{:S(2)}) %collective-permute-start) | collective-permute-done | bytes 524320 | tf_op jit(solution)/shard_map/while/body/eval_jaxpr/ppermute | solution.py:16
  192.1 7.6 %collective-permute-done.1 = bf16[2,2,128,512]{2,3,1,0:T(8,128)(2,1)} collective-permute-done((bf16[2,2,128,512]{2,3,1,0:T(8,128)(2,1)}, bf16[2,2,128,512]{2,3,1,0:T(8,128)(2,1)}, u32[]{:S(2)}, u32[]{:S(2)}) %collective-permute-start.1) | collective-permute-done | bytes 524320 | tf_op jit(solution)/shard_map/while/body/eval_jaxpr/ppermute | solution.py:55
  216.2 16.6 %collective-permute-start = (bf16[2,2,128,512]{3,2,1,0:T(8,128)(2,1)}, bf16[2,2,128,512]{3,2,1,0:T(8,128)(2,1)}, u32[]{:S(2)}, u32[]{:S(2)}) collective-permute-start(bf16[2,2,128,512]{3,2,1,0:T(8,128)(2,1)} %bitcast.168), channel_id=1, source_target_pairs={{0,4},{4,8},{8,12},{12,16},{16,20},{20,24},{24,28},{1,5},{5,9},{9,... | collective-permute-start | bytes 1572872 | tf_op jit(solution)/shard_map/while/body/eval_jaxpr/ppermute | solution.py:16
  233.2 6.1 %collective-permute-done = bf16[2,2,128,512]{3,2,1,0:T(8,128)(2,1)} collective-permute-done((bf16[2,2,128,512]{3,2,1,0:T(8,128)(2,1)}, bf16[2,2,128,512]{3,2,1,0:T(8,128)(2,1)}, u32[]{:S(2)}, u32[]{:S(2)}) %collective-permute-start) | collective-permute-done | bytes 524320 | tf_op jit(solution)/shard_map/while/body/eval_jaxpr/ppermute | solution.py:16
  247.9 7.0 %collective-permute-done.1 = bf16[2,2,128,512]{2,3,1,0:T(8,128)(2,1)} collective-permute-done((bf16[2,2,128,512]{2,3,1,0:T(8,128)(2,1)}, bf16[2,2,128,512]{2,3,1,0:T(8,128)(2,1)}, u32[]{:S(2)}, u32[]{:S(2)}) %collective-permute-start.1) | collective-permute-done | bytes 524320 | tf_op jit(solution)/shard_map/while/body/eval_jaxpr/ppermute | solution.py:55
  260.3 5.7 %collective-permute-done.3 = bf16[2,2,128,512]{2,3,1,0:T(8,128)(2,1)} collective-permute-done((bf16[2,2,128,512]{2,3,1,0:T(8,128)(2,1)}, bf16[2,2,128,512]{2,3,1,0:T(8,128)(2,1)}, u32[]{:S(2)}, u32[]{:S(2)}) %collective-permute-start.3) | collective-permute-done | bytes 524320 | tf_op jit(solution)/shard_map/while/body/eval_jaxpr/ppermute | solution.py:55
  271.3 14.8 %collective-permute-start = (bf16[2,2,128,512]{3,2,1,0:T(8,128)(2,1)}, bf16[2,2,128,512]{3,2,1,0:T(8,128)(2,1)}, u32[]{:S(2)}, u32[]{:S(2)}) collective-permute-start(bf16[2,2,128,512]{3,2,1,0:T(8,128)(2,1)} %bitcast.168), channel_id=1, source_target_pairs={{0,4},{4,8},{8,12},{12,16},{16,20},{20,24},{24,28},{1,5},{5,9},{9,... | collective-permute-start | bytes 1572872 | tf_op jit(solution)/shard_map/while/body/eval_jaxpr/ppermute | solution.py:16
  286.4 6.1 %collective-permute-done = bf16[2,2,128,512]{3,2,1,0:T(8,128)(2,1)} collective-permute-done((bf16[2,2,128,512]{3,2,1,0:T(8,128)(2,1)}, bf16[2,2,128,512]{3,2,1,0:T(8,128)(2,1)}, u32[]{:S(2)}, u32[]{:S(2)}) %collective-permute-start) | collective-permute-done | bytes 524320 | tf_op jit(solution)/shard_map/while/body/eval_jaxpr/ppermute | solution.py:16
  301.1 7.6 %collective-permute-done.1 = bf16[2,2,128,512]{2,3,1,0:T(8,128)(2,1)} collective-permute-done((bf16[2,2,128,512]{2,3,1,0:T(8,128)(2,1)}, bf16[2,2,128,512]{2,3,1,0:T(8,128)(2,1)}, u32[]{:S(2)}, u32[]{:S(2)}) %collective-permute-start.1) | collective-permute-done | bytes 524320 | tf_op jit(solution)/shard_map/while/body/eval_jaxpr/ppermute | solution.py:55
  325.1 14.2 %collective-permute-start = (bf16[2,2,128,512]{3,2,1,0:T(8,128)(2,1)}, bf16[2,2,128,512]{3,2,1,0:T(8,128)(2,1)}, u32[]{:S(2)}, u32[]{:S(2)}) collective-permute-start(bf16[2,2,128,512]{3,2,1,0:T(8,128)(2,1)} %bitcast.168), channel_id=1, source_target_pairs={{0,4},{4,8},{8,12},{12,16},{16,20},{20,24},{24,28},{1,5},{5,9},{9,... | collective-permute-start | bytes 1572872 | tf_op jit(solution)/shard_map/while/body/eval_jaxpr/ppermute | solution.py:16
  339.7 6.1 %collective-permute-done = bf16[2,2,128,512]{3,2,1,0:T(8,128)(2,1)} collective-permute-done((bf16[2,2,128,512]{3,2,1,0:T(8,128)(2,1)}, bf16[2,2,128,512]{3,2,1,0:T(8,128)(2,1)}, u32[]{:S(2)}, u32[]{:S(2)}) %collective-permute-start) | collective-permute-done | bytes 524320 | tf_op jit(solution)/shard_map/while/body/eval_jaxpr/ppermute | solution.py:16
  354.4 8.1 %collective-permute-done.1 = bf16[2,2,128,512]{2,3,1,0:T(8,128)(2,1)} collective-permute-done((bf16[2,2,128,512]{2,3,1,0:T(8,128)(2,1)}, bf16[2,2,128,512]{2,3,1,0:T(8,128)(2,1)}, u32[]{:S(2)}, u32[]{:S(2)}) %collective-permute-start.1) | collective-permute-done | bytes 524320 | tf_op jit(solution)/shard_map/while/body/eval_jaxpr/ppermute | solution.py:55
  369.2 4.5 collective-permute-done.3
  378.9 13.7 %collective-permute-start = (bf16[2,2,128,512]{3,2,1,0:T(8,128)(2,1)}, bf16[2,2,128,512]{3,2,1,0:T(8,128)(2,1)}, u32[]{:S(2)}, u32[]{:S(2)}) collective-permute-start(bf16[2,2,128,512]{3,2,1,0:T(8,128)(2,1)} %bitcast.168), channel_id=1, source_target_pairs={{0,4},{4,8},{8,12},{12,16},{16,20},{20,24},{24,28},{1,5},{5,9},{9,... | collective-permute-start | bytes 1572872 | tf_op jit(solution)/shard_map/while/body/eval_jaxpr/ppermute | solution.py:16
  393.1 6.1 %collective-permute-done = bf16[2,2,128,512]{3,2,1,0:T(8,128)(2,1)} collective-permute-done((bf16[2,2,128,512]{3,2,1,0:T(8,128)(2,1)}, bf16[2,2,128,512]{3,2,1,0:T(8,128)(2,1)}, u32[]{:S(2)}, u32[]{:S(2)}) %collective-permute-start) | collective-permute-done | bytes 524320 | tf_op jit(solution)/shard_map/while/body/eval_jaxpr/ppermute | solution.py:16
  407.8 8.6 %collective-permute-done.1 = bf16[2,2,128,512]{2,3,1,0:T(8,128)(2,1)} collective-permute-done((bf16[2,2,128,512]{2,3,1,0:T(8,128)(2,1)}, bf16[2,2,128,512]{2,3,1,0:T(8,128)(2,1)}, u32[]{:S(2)}, u32[]{:S(2)}) %collective-permute-start.1) | collective-permute-done | bytes 524320 | tf_op jit(solution)/shard_map/while/body/eval_jaxpr/ppermute | solution.py:55
  434.1 13.2 %collective-permute-start.7 = (bf16[2,1,2,128,512]{4,3,2,1,0:T(8,128)(2,1)S(1)}, bf16[2,1,2,128,512]{4,3,2,1,0:T(8,128)(2,1)S(1)}, u32[]{:S(2)}, u32[]{:S(2)}) collective-permute-start(bf16[2,1,2,128,512]{4,3,2,1,0:T(8,128)(2,1)S(1)} %convert_element_type.52), channel_id=1, source_target_pairs={{0,4},{4,8},{8,12},{12,16},{16,20},{20,24},{24,28},{1,5},{5,9},{9,... | collective-permute-start | bytes 1572872 | tf_op jit(solution)/shard_map/ppermute | solution.py:27
  448.0 8.1 %collective-permute-done.8 = bf16[2,1,2,128,512]{4,3,2,1,0:T(8,128)(2,1)S(1)} collective-permute-done((bf16[2,1,2,128,512]{4,3,2,1,0:T(8,128)(2,1)S(1)}, bf16[2,1,2,128,512]{4,3,2,1,0:T(8,128)(2,1)S(1)}, u32[]{:S(2)}, u32[]{:S(2)}) %collective-permute-start.8) | collective-permute-done | bytes 524320 | tf_op jit(solution)/shard_map/ppermute | solution.py:29
  463.0 5.4 %fusion.68 = f32[2,1,2,128,512]{4,3,2,1,0:T(8,128)S(1)} fusion(f32[2,3,2,130,512]{4,3,2,1,0:T(8,128)S(1)} %maximum_convert_fusion), kind=kLoop, calls=%fused_computation.105 | loop fusion | flops 13369344 | bytes 12779520 | tf_op jit(solution)/shard_map/add | solution.py:113
  (275 shorter events, 192.3 us)
Async XLA Ops:
  6.4 16.1 %collective-permute-start.4 = (bf16[2,2,128,512]{2,3,1,0:T(8,128)(2,1)}, bf16[2,2,128,512]{2,3,1,0:T(8,128)(2,1)}, u32[]{:S(2)}, u32[]{:S(2)}) collective-permute-start(bf16[2,2,128,512]{2,3,1,0:T(8,128)(2,1)} %get-tuple-element.103), channel_id=1, source_target_pairs={{0,1},{1,2},{2,3},{3,0},{4,5},{5,6},{6,7},{7,4},{8,9},{9,10},{10,1... | collective-permute-start | bytes 1572872 | tf_op jit(solution)/shard_map/ppermute | solution.py:55
  8.5 24.8 %collective-permute-start.5 = (bf16[2,2,128,512]{2,3,1,0:T(8,128)(2,1)}, bf16[2,2,128,512]{2,3,1,0:T(8,128)(2,1)}, u32[]{:S(2)}, u32[]{:S(2)}) collective-permute-start(bf16[2,2,128,512]{2,3,1,0:T(8,128)(2,1)} %get-tuple-element.103), channel_id=1, source_target_pairs={{0,3},{1,0},{2,1},{3,2},{4,7},{5,4},{6,5},{7,6},{8,11},{9,8},{10,9... | collective-permute-start | bytes 1572872 | tf_op jit(solution)/shard_map/ppermute | solution.py:60
  22.5 20.4 %collective-permute-start.6 = (bf16[2,2,128,512]{2,3,1,0:T(8,128)(2,1)}, bf16[2,2,128,512]{2,3,1,0:T(8,128)(2,1)}, u32[]{:S(2)}, u32[]{:S(2)}) collective-permute-start(bf16[2,2,128,512]{2,3,1,0:T(8,128)(2,1)} %collective-permute-done.4), channel_id=1, source_target_pairs={{0,1},{1,2},{2,3},{3,0},{4,5},{5,6},{6,7},{7,4},{8,9},{9,10},{10,1... | collective-permute-start | bytes 1572872 | tf_op jit(solution)/shard_map/ppermute | solution.py:55
  52.7 12.7 %collective-permute-start = (bf16[2,2,128,512]{3,2,1,0:T(8,128)(2,1)}, bf16[2,2,128,512]{3,2,1,0:T(8,128)(2,1)}, u32[]{:S(2)}, u32[]{:S(2)}) collective-permute-start(bf16[2,2,128,512]{3,2,1,0:T(8,128)(2,1)} %bitcast.168), channel_id=1, source_target_pairs={{0,4},{4,8},{8,12},{12,16},{16,20},{20,24},{24,28},{1,5},{5,9},{9,... | collective-permute-start | bytes 1572872 | tf_op jit(solution)/shard_map/while/body/eval_jaxpr/ppermute | solution.py:16
  70.8 16.1 %collective-permute-start.1 = (bf16[2,2,128,512]{2,3,1,0:T(8,128)(2,1)}, bf16[2,2,128,512]{2,3,1,0:T(8,128)(2,1)}, u32[]{:S(2)}, u32[]{:S(2)}) collective-permute-start(bf16[2,2,128,512]{2,3,1,0:T(8,128)(2,1)} %get-tuple-element.145), channel_id=1, source_target_pairs={{0,1},{1,2},{2,3},{3,0},{4,5},{5,6},{6,7},{7,4},{8,9},{9,10},{10,1... | collective-permute-start | bytes 1572872 | tf_op jit(solution)/shard_map/while/body/eval_jaxpr/ppermute | solution.py:55
  70.8 23.6 %collective-permute-start.2 = (bf16[2,2,128,512]{2,3,1,0:T(8,128)(2,1)}, bf16[2,2,128,512]{2,3,1,0:T(8,128)(2,1)}, u32[]{:S(2)}, u32[]{:S(2)}) collective-permute-start(bf16[2,2,128,512]{2,3,1,0:T(8,128)(2,1)} %get-tuple-element.145), channel_id=1, source_target_pairs={{0,3},{1,0},{2,1},{3,2},{4,7},{5,4},{6,5},{7,6},{8,11},{9,8},{10,9... | collective-permute-start | bytes 1572872 | tf_op jit(solution)/shard_map/while/body/eval_jaxpr/ppermute | solution.py:60
  86.8 16.4 %collective-permute-start.3 = (bf16[2,2,128,512]{2,3,1,0:T(8,128)(2,1)}, bf16[2,2,128,512]{2,3,1,0:T(8,128)(2,1)}, u32[]{:S(2)}, u32[]{:S(2)}) collective-permute-start(bf16[2,2,128,512]{2,3,1,0:T(8,128)(2,1)} %collective-permute-done.1), channel_id=1, source_target_pairs={{0,1},{1,2},{2,3},{3,0},{4,5},{5,6},{6,7},{7,4},{8,9},{9,10},{10,1... | collective-permute-start | bytes 1572872 | tf_op jit(solution)/shard_map/while/body/eval_jaxpr/ppermute | solution.py:55
  108.5 15.9 %collective-permute-start = (bf16[2,2,128,512]{3,2,1,0:T(8,128)(2,1)}, bf16[2,2,128,512]{3,2,1,0:T(8,128)(2,1)}, u32[]{:S(2)}, u32[]{:S(2)}) collective-permute-start(bf16[2,2,128,512]{3,2,1,0:T(8,128)(2,1)} %bitcast.168), channel_id=1, source_target_pairs={{0,4},{4,8},{8,12},{12,16},{16,20},{20,24},{24,28},{1,5},{5,9},{9,... | collective-permute-start | bytes 1572872 | tf_op jit(solution)/shard_map/while/body/eval_jaxpr/ppermute | solution.py:16
  129.8 16.1 %collective-permute-start.1 = (bf16[2,2,128,512]{2,3,1,0:T(8,128)(2,1)}, bf16[2,2,128,512]{2,3,1,0:T(8,128)(2,1)}, u32[]{:S(2)}, u32[]{:S(2)}) collective-permute-start(bf16[2,2,128,512]{2,3,1,0:T(8,128)(2,1)} %get-tuple-element.145), channel_id=1, source_target_pairs={{0,1},{1,2},{2,3},{3,0},{4,5},{5,6},{6,7},{7,4},{8,9},{9,10},{10,1... | collective-permute-start | bytes 1572872 | tf_op jit(solution)/shard_map/while/body/eval_jaxpr/ppermute | solution.py:55
  129.8 19.6 %collective-permute-start.2 = (bf16[2,2,128,512]{2,3,1,0:T(8,128)(2,1)}, bf16[2,2,128,512]{2,3,1,0:T(8,128)(2,1)}, u32[]{:S(2)}, u32[]{:S(2)}) collective-permute-start(bf16[2,2,128,512]{2,3,1,0:T(8,128)(2,1)} %get-tuple-element.145), channel_id=1, source_target_pairs={{0,3},{1,0},{2,1},{3,2},{4,7},{5,4},{6,5},{7,6},{8,11},{9,8},{10,9... | collective-permute-start | bytes 1572872 | tf_op jit(solution)/shard_map/while/body/eval_jaxpr/ppermute | solution.py:60
  145.9 11.1 %collective-permute-start.3 = (bf16[2,2,128,512]{2,3,1,0:T(8,128)(2,1)}, bf16[2,2,128,512]{2,3,1,0:T(8,128)(2,1)}, u32[]{:S(2)}, u32[]{:S(2)}) collective-permute-start(bf16[2,2,128,512]{2,3,1,0:T(8,128)(2,1)} %collective-permute-done.1), channel_id=1, source_target_pairs={{0,1},{1,2},{2,3},{3,0},{4,5},{5,6},{6,7},{7,4},{8,9},{9,10},{10,1... | collective-permute-start | bytes 1572872 | tf_op jit(solution)/shard_map/while/body/eval_jaxpr/ppermute | solution.py:55
  162.3 21.2 %collective-permute-start = (bf16[2,2,128,512]{3,2,1,0:T(8,128)(2,1)}, bf16[2,2,128,512]{3,2,1,0:T(8,128)(2,1)}, u32[]{:S(2)}, u32[]{:S(2)}) collective-permute-start(bf16[2,2,128,512]{3,2,1,0:T(8,128)(2,1)} %bitcast.168), channel_id=1, source_target_pairs={{0,4},{4,8},{8,12},{12,16},{16,20},{20,24},{24,28},{1,5},{5,9},{9,... | collective-permute-start | bytes 1572872 | tf_op jit(solution)/shard_map/while/body/eval_jaxpr/ppermute | solution.py:16
  188.8 10.9 %collective-permute-start.1 = (bf16[2,2,128,512]{2,3,1,0:T(8,128)(2,1)}, bf16[2,2,128,512]{2,3,1,0:T(8,128)(2,1)}, u32[]{:S(2)}, u32[]{:S(2)}) collective-permute-start(bf16[2,2,128,512]{2,3,1,0:T(8,128)(2,1)} %get-tuple-element.145), channel_id=1, source_target_pairs={{0,1},{1,2},{2,3},{3,0},{4,5},{5,6},{6,7},{7,4},{8,9},{9,10},{10,1... | collective-permute-start | bytes 1572872 | tf_op jit(solution)/shard_map/while/body/eval_jaxpr/ppermute | solution.py:55
  188.8 16.4 %collective-permute-start.2 = (bf16[2,2,128,512]{2,3,1,0:T(8,128)(2,1)}, bf16[2,2,128,512]{2,3,1,0:T(8,128)(2,1)}, u32[]{:S(2)}, u32[]{:S(2)}) collective-permute-start(bf16[2,2,128,512]{2,3,1,0:T(8,128)(2,1)} %get-tuple-element.145), channel_id=1, source_target_pairs={{0,3},{1,0},{2,1},{3,2},{4,7},{5,4},{6,5},{7,6},{8,11},{9,8},{10,9... | collective-permute-start | bytes 1572872 | tf_op jit(solution)/shard_map/while/body/eval_jaxpr/ppermute | solution.py:60
  199.7 11.1 %collective-permute-start.3 = (bf16[2,2,128,512]{2,3,1,0:T(8,128)(2,1)}, bf16[2,2,128,512]{2,3,1,0:T(8,128)(2,1)}, u32[]{:S(2)}, u32[]{:S(2)}) collective-permute-start(bf16[2,2,128,512]{2,3,1,0:T(8,128)(2,1)} %collective-permute-done.1), channel_id=1, source_target_pairs={{0,1},{1,2},{2,3},{3,0},{4,5},{5,6},{6,7},{7,4},{8,9},{9,10},{10,1... | collective-permute-start | bytes 1572872 | tf_op jit(solution)/shard_map/while/body/eval_jaxpr/ppermute | solution.py:55
  216.2 23.1 %collective-permute-start = (bf16[2,2,128,512]{3,2,1,0:T(8,128)(2,1)}, bf16[2,2,128,512]{3,2,1,0:T(8,128)(2,1)}, u32[]{:S(2)}, u32[]{:S(2)}) collective-permute-start(bf16[2,2,128,512]{3,2,1,0:T(8,128)(2,1)} %bitcast.168), channel_id=1, source_target_pairs={{0,4},{4,8},{8,12},{12,16},{16,20},{20,24},{24,28},{1,5},{5,9},{9,... | collective-permute-start | bytes 1572872 | tf_op jit(solution)/shard_map/while/body/eval_jaxpr/ppermute | solution.py:16
  244.6 14.6 %collective-permute-start.2 = (bf16[2,2,128,512]{2,3,1,0:T(8,128)(2,1)}, bf16[2,2,128,512]{2,3,1,0:T(8,128)(2,1)}, u32[]{:S(2)}, u32[]{:S(2)}) collective-permute-start(bf16[2,2,128,512]{2,3,1,0:T(8,128)(2,1)} %get-tuple-element.145), channel_id=1, source_target_pairs={{0,3},{1,0},{2,1},{3,2},{4,7},{5,4},{6,5},{7,6},{8,11},{9,8},{10,9... | collective-permute-start | bytes 1572872 | tf_op jit(solution)/shard_map/while/body/eval_jaxpr/ppermute | solution.py:60
  254.8 11.2 %collective-permute-start.3 = (bf16[2,2,128,512]{2,3,1,0:T(8,128)(2,1)}, bf16[2,2,128,512]{2,3,1,0:T(8,128)(2,1)}, u32[]{:S(2)}, u32[]{:S(2)}) collective-permute-start(bf16[2,2,128,512]{2,3,1,0:T(8,128)(2,1)} %collective-permute-done.1), channel_id=1, source_target_pairs={{0,1},{1,2},{2,3},{3,0},{4,5},{5,6},{6,7},{7,4},{8,9},{9,10},{10,1... | collective-permute-start | bytes 1572872 | tf_op jit(solution)/shard_map/while/body/eval_jaxpr/ppermute | solution.py:55
  271.3 21.2 %collective-permute-start = (bf16[2,2,128,512]{3,2,1,0:T(8,128)(2,1)}, bf16[2,2,128,512]{3,2,1,0:T(8,128)(2,1)}, u32[]{:S(2)}, u32[]{:S(2)}) collective-permute-start(bf16[2,2,128,512]{3,2,1,0:T(8,128)(2,1)} %bitcast.168), channel_id=1, source_target_pairs={{0,4},{4,8},{8,12},{12,16},{16,20},{20,24},{24,28},{1,5},{5,9},{9,... | collective-permute-start | bytes 1572872 | tf_op jit(solution)/shard_map/while/body/eval_jaxpr/ppermute | solution.py:16
  297.9 10.9 %collective-permute-start.1 = (bf16[2,2,128,512]{2,3,1,0:T(8,128)(2,1)}, bf16[2,2,128,512]{2,3,1,0:T(8,128)(2,1)}, u32[]{:S(2)}, u32[]{:S(2)}) collective-permute-start(bf16[2,2,128,512]{2,3,1,0:T(8,128)(2,1)} %get-tuple-element.145), channel_id=1, source_target_pairs={{0,1},{1,2},{2,3},{3,0},{4,5},{5,6},{6,7},{7,4},{8,9},{9,10},{10,1... | collective-permute-start | bytes 1572872 | tf_op jit(solution)/shard_map/while/body/eval_jaxpr/ppermute | solution.py:55
  297.9 16.4 %collective-permute-start.2 = (bf16[2,2,128,512]{2,3,1,0:T(8,128)(2,1)}, bf16[2,2,128,512]{2,3,1,0:T(8,128)(2,1)}, u32[]{:S(2)}, u32[]{:S(2)}) collective-permute-start(bf16[2,2,128,512]{2,3,1,0:T(8,128)(2,1)} %get-tuple-element.145), channel_id=1, source_target_pairs={{0,3},{1,0},{2,1},{3,2},{4,7},{5,4},{6,5},{7,6},{8,11},{9,8},{10,9... | collective-permute-start | bytes 1572872 | tf_op jit(solution)/shard_map/while/body/eval_jaxpr/ppermute | solution.py:60
  308.7 11.1 %collective-permute-start.3 = (bf16[2,2,128,512]{2,3,1,0:T(8,128)(2,1)}, bf16[2,2,128,512]{2,3,1,0:T(8,128)(2,1)}, u32[]{:S(2)}, u32[]{:S(2)}) collective-permute-start(bf16[2,2,128,512]{2,3,1,0:T(8,128)(2,1)} %collective-permute-done.1), channel_id=1, source_target_pairs={{0,1},{1,2},{2,3},{3,0},{4,5},{5,6},{6,7},{7,4},{8,9},{9,10},{10,1... | collective-permute-start | bytes 1572872 | tf_op jit(solution)/shard_map/while/body/eval_jaxpr/ppermute | solution.py:55
  325.1 20.7 %collective-permute-start = (bf16[2,2,128,512]{3,2,1,0:T(8,128)(2,1)}, bf16[2,2,128,512]{3,2,1,0:T(8,128)(2,1)}, u32[]{:S(2)}, u32[]{:S(2)}) collective-permute-start(bf16[2,2,128,512]{3,2,1,0:T(8,128)(2,1)} %bitcast.168), channel_id=1, source_target_pairs={{0,4},{4,8},{8,12},{12,16},{16,20},{20,24},{24,28},{1,5},{5,9},{9,... | collective-permute-start | bytes 1572872 | tf_op jit(solution)/shard_map/while/body/eval_jaxpr/ppermute | solution.py:16
  351.2 11.3 %collective-permute-start.1 = (bf16[2,2,128,512]{2,3,1,0:T(8,128)(2,1)}, bf16[2,2,128,512]{2,3,1,0:T(8,128)(2,1)}, u32[]{:S(2)}, u32[]{:S(2)}) collective-permute-start(bf16[2,2,128,512]{2,3,1,0:T(8,128)(2,1)} %get-tuple-element.145), channel_id=1, source_target_pairs={{0,1},{1,2},{2,3},{3,0},{4,5},{5,6},{6,7},{7,4},{8,9},{9,10},{10,1... | collective-permute-start | bytes 1572872 | tf_op jit(solution)/shard_map/while/body/eval_jaxpr/ppermute | solution.py:55
  351.2 16.8 %collective-permute-start.2 = (bf16[2,2,128,512]{2,3,1,0:T(8,128)(2,1)}, bf16[2,2,128,512]{2,3,1,0:T(8,128)(2,1)}, u32[]{:S(2)}, u32[]{:S(2)}) collective-permute-start(bf16[2,2,128,512]{2,3,1,0:T(8,128)(2,1)} %get-tuple-element.145), channel_id=1, source_target_pairs={{0,3},{1,0},{2,1},{3,2},{4,7},{5,4},{6,5},{7,6},{8,11},{9,8},{10,9... | collective-permute-start | bytes 1572872 | tf_op jit(solution)/shard_map/while/body/eval_jaxpr/ppermute | solution.py:60
  362.5 11.2 %collective-permute-start.3 = (bf16[2,2,128,512]{2,3,1,0:T(8,128)(2,1)}, bf16[2,2,128,512]{2,3,1,0:T(8,128)(2,1)}, u32[]{:S(2)}, u32[]{:S(2)}) collective-permute-start(bf16[2,2,128,512]{2,3,1,0:T(8,128)(2,1)} %collective-permute-done.1), channel_id=1, source_target_pairs={{0,1},{1,2},{2,3},{3,0},{4,5},{5,6},{6,7},{7,4},{8,9},{9,10},{10,1... | collective-permute-start | bytes 1572872 | tf_op jit(solution)/shard_map/while/body/eval_jaxpr/ppermute | solution.py:55
  378.9 20.2 %collective-permute-start = (bf16[2,2,128,512]{3,2,1,0:T(8,128)(2,1)}, bf16[2,2,128,512]{3,2,1,0:T(8,128)(2,1)}, u32[]{:S(2)}, u32[]{:S(2)}) collective-permute-start(bf16[2,2,128,512]{3,2,1,0:T(8,128)(2,1)} %bitcast.168), channel_id=1, source_target_pairs={{0,4},{4,8},{8,12},{12,16},{16,20},{20,24},{24,28},{1,5},{5,9},{9,... | collective-permute-start | bytes 1572872 | tf_op jit(solution)/shard_map/while/body/eval_jaxpr/ppermute | solution.py:16
  404.5 11.8 %collective-permute-start.1 = (bf16[2,2,128,512]{2,3,1,0:T(8,128)(2,1)}, bf16[2,2,128,512]{2,3,1,0:T(8,128)(2,1)}, u32[]{:S(2)}, u32[]{:S(2)}) collective-permute-start(bf16[2,2,128,512]{2,3,1,0:T(8,128)(2,1)} %get-tuple-element.145), channel_id=1, source_target_pairs={{0,1},{1,2},{2,3},{3,0},{4,5},{5,6},{6,7},{7,4},{8,9},{9,10},{10,1... | collective-permute-start | bytes 1572872 | tf_op jit(solution)/shard_map/while/body/eval_jaxpr/ppermute | solution.py:55
  404.5 17.3 %collective-permute-start.2 = (bf16[2,2,128,512]{2,3,1,0:T(8,128)(2,1)}, bf16[2,2,128,512]{2,3,1,0:T(8,128)(2,1)}, u32[]{:S(2)}, u32[]{:S(2)}) collective-permute-start(bf16[2,2,128,512]{2,3,1,0:T(8,128)(2,1)} %get-tuple-element.145), channel_id=1, source_target_pairs={{0,3},{1,0},{2,1},{3,2},{4,7},{5,4},{6,5},{7,6},{8,11},{9,8},{10,9... | collective-permute-start | bytes 1572872 | tf_op jit(solution)/shard_map/while/body/eval_jaxpr/ppermute | solution.py:60
  416.3 11.2 %collective-permute-start.3 = (bf16[2,2,128,512]{2,3,1,0:T(8,128)(2,1)}, bf16[2,2,128,512]{2,3,1,0:T(8,128)(2,1)}, u32[]{:S(2)}, u32[]{:S(2)}) collective-permute-start(bf16[2,2,128,512]{2,3,1,0:T(8,128)(2,1)} %collective-permute-done.1), channel_id=1, source_target_pairs={{0,1},{1,2},{2,3},{3,0},{4,5},{5,6},{6,7},{7,4},{8,9},{9,10},{10,1... | collective-permute-start | bytes 1572872 | tf_op jit(solution)/shard_map/while/body/eval_jaxpr/ppermute | solution.py:55
  432.1 24.1 %collective-permute-start.8 = (bf16[2,1,2,128,512]{4,3,2,1,0:T(8,128)(2,1)S(1)}, bf16[2,1,2,128,512]{4,3,2,1,0:T(8,128)(2,1)S(1)}, u32[]{:S(2)}, u32[]{:S(2)}) collective-permute-start(bf16[2,1,2,128,512]{4,3,2,1,0:T(8,128)(2,1)S(1)} %convert_element_type.52), channel_id=1, source_target_pairs={{4,0},{8,4},{12,8},{16,12},{20,16},{24,20},{28,24},{5,1},{9,5},{13... | collective-permute-start | bytes 1572872 | tf_op jit(solution)/shard_map/ppermute | solution.py:29
  434.1 22.0 %collective-permute-start.7 = (bf16[2,1,2,128,512]{4,3,2,1,0:T(8,128)(2,1)S(1)}, bf16[2,1,2,128,512]{4,3,2,1,0:T(8,128)(2,1)S(1)}, u32[]{:S(2)}, u32[]{:S(2)}) collective-permute-start(bf16[2,1,2,128,512]{4,3,2,1,0:T(8,128)(2,1)S(1)} %convert_element_type.52), channel_id=1, source_target_pairs={{0,4},{4,8},{8,12},{12,16},{16,20},{20,24},{24,28},{1,5},{5,9},{9,... | collective-permute-start | bytes 1572872 | tf_op jit(solution)/shard_map/ppermute | solution.py:27
  (37 other events, 425.0 us)
